TPU v7x, 128 devices: a whole 4x4x4 slice. The times are simulated.
128 devices in a mesh: front: 8 (over z, core), panel: 16 (over x, y).
Axes of the slice: x: 4, y: 4, z: 4, core: 2. Of those that a mesh axis runs over, the one named last changes fastest.
Arguments:
- pivot_columns: float32 [8, 8192, 1024], P('front', 'panel')
- child_rows: bfloat16 [8, 16, 16, 4, 8192], P('front', 'panel'), may hold values from -0.375 to 0.375
- slot_rows: int32 [8, 16, 16, 4], P('front', 'panel'), may hold values from -1 to 511, as said below
- parents: int32 [8], replicated, may hold values from 0 to 7, as said below
- pivot_rhs: float32 [8, 1024, 128], P('front'), may hold values from -6 to 6
- boundary_solution: float32 [8, 8192, 128], P('front', 'panel'), may hold values from -6 to 6
Outputs:
- panel_factor: float32 [8, 8192, 1024], P('front', 'panel')
- update_matrix: bfloat16 [8, 8192, 7168], P('front', 'panel')
- front_solution: float32 [8, 8192, 128], P('front', 'panel')
- child_solution: float32 [8, 16, 16, 4, 128], P('front', 'panel')
Inputs may be any that keep to these rules, and one draw needn't show every extreme that they name: parents[c] is the front of this level into which child front c's rows are added; a front may take several children or none. `slot_rows`: the live slots of each tile of 4 slots come first; the rows that one child front sends to one destination device are distinct; for each child front one destination device receives full tiles from every source device.
All inputs are finite; a program needn't handle non-finite values.
Results may differ from a plain program's by a relative error of at most 0.007.
Values may be sent and summed in bfloat16 or wider, within the bound.
A program may use at most 192 MiB of HBM per device.

v0:
```python
import jax
import jax.numpy as jnp
from jax import lax
from jax.sharding import PartitionSpec as P

K = 512
NSTEP = 2


def spread(shard, axis, root):
    mine = lax.axis_index(axis) == root
    return lax.psum(jnp.where(mine, shard, jnp.zeros_like(shard)), axis)


def outer_rows(mine, piece):
    return lax.dot_general(
        mine, piece, (((1,), (1,)), ((), ())), preferred_element_type=jnp.float32
    )


def scatter_term(slots, rows, local_ids, width):
    onehot = (slots.reshape(-1)[None, :] == local_ids[:, None]).astype(jnp.bfloat16)
    return jnp.dot(onehot, rows.reshape(-1, width), preferred_element_type=jnp.float32)


def on_device(pivot_columns, child_rows, slot_rows, parents, pivot_rhs, boundary_solution):
    highest = lax.Precision.HIGHEST
    panel_index = lax.axis_index("panel")
    front_index = lax.axis_index("front")
    piv_cols = pivot_columns[0]
    row_count = piv_cols.shape[0]
    pivots = piv_cols.shape[1]
    width = child_rows.shape[-1]
    rhs_count = pivot_rhs.shape[-1]
    local_ids = jnp.arange(row_count, dtype=jnp.int32)
    glob_rows = panel_index * row_count + local_ids
    rows_out = child_rows[0, 0]
    slots_out = slot_rows[0, 0]
    routed_rows, routed_slots = (
        lax.all_to_all(rows_out, "panel", split_axis=0, concat_axis=0, tiled=True),
        lax.all_to_all(slots_out, "panel", split_axis=0, concat_axis=0, tiled=True),
    )
    piece_rows = lax.all_gather(routed_rows[None], "front", axis=0, tiled=True)
    piece_slots = lax.all_gather(routed_slots[None], "front", axis=0, tiled=True)
    keeping = parents == front_index

    def add_rows(current):
        kept_slots = jnp.where(keeping[:, None, None], piece_slots, -1)
        return scatter_term(kept_slots, piece_rows, local_ids, width)

    def keep_same(current):
        return current

    assembled = lax.cond(
        jnp.any(keeping), add_rows, keep_same, jnp.zeros((row_count, width), jnp.float32)
    )
    work = assembled + jnp.concatenate(
        [piv_cols, jnp.zeros((row_count, width - pivots), jnp.float32)], axis=1
    )
    identity_block = jnp.eye(K, dtype=jnp.float32)

    def factor_block(values):
        lower = jnp.linalg.cholesky(values)
        return lax.linalg.triangular_solve(lower, identity_block, left_side=True, lower=True)

    def empty_block(values):
        return jnp.zeros_like(values)

    factors = []
    inverses = []
    for panel_step in range(NSTEP):
        low_edge = panel_step * K
        high_edge = low_edge + K
        root_rank = low_edge // row_count
        offset = low_edge - root_rank * row_count
        pivot_block = work[offset : offset + K, low_edge:high_edge]
        inverse = lax.cond(panel_index == root_rank, factor_block, empty_block, pivot_block)
        inverse = spread(inverse, "panel", root_rank)
        column = jnp.dot(work[:, low_edge:high_edge], inverse.T, precision=highest)
        column = jnp.where(glob_rows[:, None] >= low_edge, column, 0.0)
        packed = column.astype(jnp.bfloat16)
        factors.append(column)
        inverses.append(inverse)
        work = work - outer_rows(packed, lax.all_gather(packed, "panel", axis=0, tiled=True))
    factor_all = jnp.concatenate(factors, axis=1)
    trailing = work[:, pivots:]
    update_matrix = jnp.where(glob_rows[:, None] >= pivots, trailing, 0.0).astype(jnp.bfloat16)
    known = boundary_solution[0]
    right_side = pivot_rhs[0]

    def local_values(solved):
        extended = jnp.concatenate([solved, jnp.zeros((row_count, rhs_count), jnp.float32)], axis=0)
        begin = jnp.minimum(panel_index * row_count, pivots)
        segment = lax.dynamic_slice_in_dim(extended, begin, row_count)
        return jnp.where(glob_rows[:, None] < pivots, segment, known)

    solved = jnp.zeros((pivots, rhs_count), jnp.float32)
    contract_rows = (((0,), (0,)), ((), ()))
    for panel_step in reversed(range(NSTEP)):
        low_edge = panel_step * K
        high_edge = low_edge + K
        current = local_values(solved)
        masked = jnp.where(glob_rows[:, None] >= high_edge, factors[panel_step], 0.0)
        partial_sum = lax.dot_general(masked, current, contract_rows, precision=highest)
        carried = lax.psum(partial_sum, "panel")
        value = lax.dot_general(
            inverses[panel_step],
            right_side[low_edge:high_edge] - carried,
            contract_rows,
            precision=highest,
        )
        solved = solved.at[low_edge:high_edge].set(value)
    front_values = local_values(solved)
    slot_onehot = (routed_slots[..., None] == local_ids).astype(jnp.float32)
    piece = lax.all_gather(front_values[None], "front", axis=0, tiled=True)
    piece_count = piece.shape[0]
    weights = (jnp.arange(piece_count, dtype=jnp.int32) == parents[front_index]).astype(jnp.float32)
    chosen = jnp.einsum("n,nrh->rh", weights, piece, precision=highest)
    slot_values = jnp.einsum("psr,rh->psh", slot_onehot, chosen, precision=highest)
    child_values = lax.all_to_all(slot_values, "panel", split_axis=0, concat_axis=0, tiled=True)
    return (factor_all[None], update_matrix[None], front_values[None], child_values[None, None])


def solution(mesh):
    in_specs = (
        P("front", "panel", None),
        P("front", "panel", None, None, None),
        P("front", "panel", None, None),
        P(),
        P("front", None, None),
        P("front", "panel", None),
    )
    out_specs = (
        P("front", "panel", None),
        P("front", "panel", None),
        P("front", "panel", None),
        P("front", "panel", None, None, None),
    )
    return jax.shard_map(
        on_device, mesh=mesh, in_specs=in_specs, out_specs=out_specs, check_vma=False
    )
```

profile of v0, /device:TPU:0, one launch (start us, length us, event | category | flops | bytes accessed | tf_op | source)
XLA Modules:
  0.0 1002.9 jit_solution(4517287727802942974)
XLA Ops:
  7.2 24.1 %all_to_all.19 = bf16[16,4,8192]{2,1,0:T(4,128)(2,1)} all-to-all(bf16[16,4,8192]{2,1,0:T(4,128)(2,1)} %bitcast.145), channel_id=1, replica_groups=mesh['front'=8,'panel'=16] {'panel'}, dimensions={0} | all-to-all | bytes 2097152 | tf_op jit(solution)/shard_map/all_to_all | solution.py:40
  38.6 5.4 all-to-all-done
  44.0 14.0 %all-gather = s32[128,1,4]{2,1,0:T(1,128)S(1)} all-gather(s32[16,1,4]{2,1,0:T(1,128)S(1)} %all-to-all-done), channel_id=2, replica_groups=mesh['front'=8,'panel'=16] {'front'}, dimensions={0}, use_global_device_ids=true | all-gather | bytes 2304 | tf_op jit(solution)/shard_map/all_gather | solution.py:44
  58.0 22.9 %all-gather.12.cloned.1.call-done = bf16[128,4,8192]{2,1,0:T(4,128)(2,1)} async-done(((bf16[16,4,8192]{2,1,0:T(4,128)(2,1)}), bf16[128,4,8192]{2,1,0:T(4,128)(2,1)}) %all-gather.12.cloned.1.call-update) | async-done | bytes 8388624 | tf_op jit(solution)/shard_map/all_gather | solution.py:43
  80.9 24.2 %conditional.3 = (f32[512,8192]{1,0:T(8,128)}) conditional(s32[]{:T(128)} %convert_element_type.26, () %tuple.36, (pred[8]{0:T(512)(128)(4,1)S(1)}, s32[8,16,4]{2,1,0:T(8,128)S(1)}, s32[512]{0:T(512)S(1)}, bf16[8,16,4,8192]{3,2,1,0:T(4,128)(2,1)}) %tuple.137), branch_computations={%region_1.0_spmd, %region_2.3_spmd} | conditional | flops 4295229952 | bytes 41955344 | solution.py:54
  81.0 12.5 %reshape.120 = bf16[512,8192]{1,0:T(8,128)(2,1)} reshape(bf16[8,16,4,8192]{3,2,1,0:T(4,128)(2,1)} %get-tuple-element.54) | data formatting | bytes 16777216 | tf_op jit(solution)/shard_map/cond/branch_1_fun/reshape | solution.py:23
  93.6 11.5 %fusion = f32[512,8192]{1,0:T(8,128)} fusion(bf16[512,8192]{1,0:T(8,128)(2,1)} %reshape.120, s32[512]{0:T(512)S(1)} %eq.3, s32[512]{0:T(512)S(1)} %get-tuple-element.53), kind=kOutput, calls=%fused_computation | convolution fusion | flops 4295229440 | bytes 25169920 | tf_op jit(solution)/shard_map/cond/branch_1_fun/dot_general | solution.py:23
  105.0 7.0 pad_add_fusion
  112.0 5.7 copy-done
  117.8 141.4 %conditional.4 = (f32[512,512]{0,1:T(8,128)}) conditional(s32[]{:T(128)} %convert_element_type.27, () %tuple.38, (f32[512,512]{1,0:T(8,128)S(1)}, f32[512,512]{1,0:T(8,128)S(1)}) %tuple.39), branch_computations={%region_3.4_spmd, %region_4.15_spmd} | conditional | flops 1412760064 | bytes 26743068 | solution.py:77
  119.7 11.7 %cholesky.286 = f32[128,128]{1,0:T(8,128)S(1)} custom-call(f32[128,128]{1,0:T(8,128)S(1)} %cholesky.426), custom_call_target="Cholesky" | custom-call | tf_op jit(solution)/shard_map/cond/branch_1_fun/jit(cholesky)/cholesky | solution.py:63
  131.4 9.8 custom-call.27
  143.9 11.7 %cholesky.305 = f32[128,128]{1,0:T(8,128)S(1)} custom-call(f32[128,128]{1,0:T(8,128)S(1)} %cholesky.430), custom_call_target="Cholesky" | custom-call | tf_op jit(solution)/shard_map/cond/branch_1_fun/jit(cholesky)/cholesky | solution.py:63
  157.7 10.0 %custom-call.28 = f32[1,128,128]{1,2,0:T(8,128)S(1)} custom-call(f32[1,128,128]{2,1,0:T(8,128)S(1)} %get-tuple-element.139), custom_call_target="InvertDiagBlocksLowerTriangular" | custom-call | tf_op jit(solution)/shard_map/cond/branch_1_fun/jit(cholesky)/cholesky | solution.py:63
  169.3 11.7 %cholesky.326 = f32[128,128]{1,0:T(8,128)S(1)} custom-call(f32[128,128]{1,0:T(8,128)S(1)} %cholesky.435), custom_call_target="Cholesky" | custom-call | tf_op jit(solution)/shard_map/cond/branch_1_fun/jit(cholesky)/cholesky | solution.py:63
  182.3 9.8 custom-call.29
  193.6 11.7 %cholesky.343 = f32[128,128]{1,0:T(8,128)S(1)} custom-call(f32[128,128]{1,0:T(8,128)S(1)} %convolution_subtract_fusion.5), custom_call_target="Cholesky" | custom-call | tf_op jit(solution)/shard_map/cond/branch_1_fun/jit(cholesky)/cholesky | solution.py:63
  207.2 8.0 while.6
  215.3 39.3 %custom-call.30 = f32[4,128,128]{1,2,0:T(8,128)S(1)} custom-call(f32[4,128,128]{2,1,0:T(8,128)S(1)} %get-tuple-element.77), custom_call_target="InvertDiagBlocksLowerTriangular" | custom-call | tf_op jit(solution)/shard_map/cond/branch_1_fun/triangular_solve/custom-call.3 | solution.py:64
  261.7 82.1 %all-reduce.11.cloned.1.call-done = f32[512,512]{0,1:T(8,128)} async-done(((f32[512,512]{0,1:T(8,128)}), f32[512,512]{0,1:T(8,128)}) %all-reduce.11.cloned.1.call-update) | async-done | bytes 1048592 | tf_op jit(solution)/shard_map/psum | solution.py:12
  348.1 77.5 %all-gather.8.cloned.1.call-done = bf16[8192,512]{0,1:T(8,128)(2,1)} async-done(((bf16[512,512]{0,1:T(8,128)(2,1)}), bf16[8192,512]{0,1:T(8,128)(2,1)}) %all-gather.8.cloned.1.call-update) | async-done | bytes 8388624 | tf_op jit(solution)/shard_map/all_gather | solution.py:84
  425.6 18.7 %convolution_subtract_fusion.12 = f32[512,8192]{1,0:T(8,128)} fusion(f32[512,8192]{1,0:T(8,128)} %copy-done, bf16[512,512]{0,1:T(8,128)(2,1)} %get-tuple-element.163, bf16[8192,512]{0,1:T(8,128)(2,1)} %all-gather.8.cloned.1.call-done), kind=kOutput, calls=%fused_computation.141 | convolution fusion | flops 4299161600 | bytes 42467328 | tf_op jit(solution)/shard_map/dot_general | solution.py:16
  445.6 8.3 conditional.5
  455.1 237.6 %all-reduce.13.cloned.1.call-done = f32[512,512]{0,1:T(8,128)} async-done(((f32[512,512]{0,1:T(8,128)}), f32[512,512]{0,1:T(8,128)}) %all-reduce.13.cloned.1.call-update) | async-done | bytes 1048592 | tf_op jit(solution)/shard_map/psum | solution.py:12
  698.8 83.3 %all-reduce.15.cloned.1.call-done = f32[512,128]{1,0:T(8,128)} async-done(((f32[512,128]{1,0:T(8,128)}), f32[512,128]{1,0:T(8,128)}) %all-reduce.15.cloned.1.call-update) | async-done | bytes 262160 | tf_op jit(solution)/shard_map/psum | solution.py:105
  786.3 83.5 %all-reduce.17.cloned.1.call-done = f32[512,128]{1,0:T(8,128)} async-done(((f32[512,128]{1,0:T(8,128)}), f32[512,128]{1,0:T(8,128)}) %all-reduce.17.cloned.1.call-update) | async-done | bytes 262160 | tf_op jit(solution)/shard_map/psum | solution.py:105
  874.5 23.5 %all-gather.14.cloned.1.call-done = f32[4096,128]{1,0:T(8,128)} async-done(((f32[512,128]{1,0:T(8,128)}), f32[4096,128]{1,0:T(8,128)}) %all-gather.14.cloned.1.call-update) | async-done | bytes 2097168 | tf_op jit(solution)/shard_map/all_gather | solution.py:115
  898.0 4.4 fusion.67
  903.3 7.1 all-to-all-start.2
  918.0 60.9 %all-gather.10.cloned.1.call-done = bf16[8192,512]{0,1:T(8,128)(2,1)} async-done(((bf16[512,512]{0,1:T(8,128)(2,1)}), bf16[8192,512]{0,1:T(8,128)(2,1)}) %all-gather.10.cloned.1.call-update) | async-done | bytes 8388624 | tf_op jit(solution)/shard_map/all_gather | solution.py:84
  978.8 7.1 fusion.112
  986.0 9.0 fusion.66
  (104 shorter events, 63.4 us)
Async XLA Ops:
  7.2 73.7 %all-gather.12.cloned.1.call-start = ((), (), s32[]{:S(2)}) async-start(), calls=%async_computation.9 | async-start | bytes 9437184 | tf_op jit(solution)/shard_map/all_gather | solution.py:43
  32.7 11.3 %all-to-all-start = ((s32[16,1,4]{2,1,0:T(1,128)}), s32[16,1,4]{2,1,0:T(1,128)S(1)}, u32[]{:S(2)}, u32[]{:S(2)}) async-start(s32[16,1,4]{2,1,0:T(1,128)} %copy.30), calls=%async_computation | async-start | bytes 16384 | tf_op jit(solution)/shard_map/all_to_all | solution.py:41
  36.5 307.3 %all-reduce.11.cloned.1.call-start = ((), (), s32[]{:S(2)}) async-start(), calls=%async_computation.3 | async-start | bytes 2097152 | tf_op jit(solution)/shard_map/psum | solution.py:12
  112.0 5.7 copy-start
  118.7 1.0 copy-start.2
  261.6 164.0 %all-gather.8.cloned.1.call-start = ((), (), s32[]{:S(2)}) async-start(), calls=%async_computation.4 | async-start | bytes 8912896 | tf_op jit(solution)/shard_map/all_gather | solution.py:84
  348.0 344.7 %all-reduce.13.cloned.1.call-start = ((), (), s32[]{:S(2)}) async-start(), calls=%async_computation.5 | async-start | bytes 2097152 | tf_op jit(solution)/shard_map/psum | solution.py:12
  445.6 251.4 %copy-start.4 = (f32[1,512,128]{2,1,0:T(8,128)S(1)}, f32[1,512,128]{2,1,0:T(8,128)}, u32[]{:S(2)}) copy-start(f32[1,512,128]{2,1,0:T(8,128)} %param.24) | copy-start | bytes 786436
  453.8 328.3 %copy-start.6 = (f32[1,1024,128]{2,1,0:T(8,128)S(1)}, f32[1,1024,128]{2,1,0:T(8,128)}, u32[]{:S(2)}) copy-start(f32[1,1024,128]{2,1,0:T(8,128)} %param.23) | copy-start | bytes 1572868
  453.8 419.9 %copy-start.7 = (s32[8]{0:T(128)S(1)}, s32[8]{0:T(128)}, u32[]{:S(2)}) copy-start(s32[8]{0:T(128)} %param.22) | copy-start | bytes 100
  454.9 327.2 %all-reduce.15.cloned.1.call-start = ((), (), s32[]{:S(2)}) async-start(), calls=%async_computation.7 | async-start | bytes 524288 | tf_op jit(solution)/shard_map/psum | solution.py:105
  698.8 171.0 %all-reduce.17.cloned.1.call-start = ((), (), s32[]{:S(2)}) async-start(), calls=%async_computation.8 | async-start | bytes 524288 | tf_op jit(solution)/shard_map/psum | solution.py:105
  784.4 194.4 %copy-start.1 = (bf16[512,512]{0,1:T(8,128)(2,1)S(1)}, bf16[512,512]{0,1:T(8,128)(2,1)}, u32[]{:S(2)}) copy-start(bf16[512,512]{0,1:T(8,128)(2,1)} %get-tuple-element.165) | copy-start | bytes 1572868
  786.2 111.8 %all-gather.14.cloned.1.call-start = ((), (), s32[]{:S(2)}) async-start(), calls=%async_computation.10 | async-start | bytes 2359296 | tf_op jit(solution)/shard_map/all_gather | solution.py:115
  873.0 105.8 %all-gather.10.cloned.1.call-start = ((), (), s32[]{:S(2)}) async-start(), calls=%async_computation.6 | async-start | bytes 8912896 | tf_op jit(solution)/shard_map/all_gather | solution.py:84
  903.3 14.6 %all-to-all-start.2 = ((f32[16,4,128]{2,1,0:T(4,128)}), f32[16,4,128]{2,1,0:T(4,128)S(1)}, u32[]{:S(2)}, u32[]{:S(2)}) async-start(f32[16,4,128]{2,1,0:T(4,128)} %copy.36), calls=%async_computation.2 | async-start | bytes 65536 | tf_op jit(solution)/shard_map/all_to_all | solution.py:120
Sparse Core Ops, SparseCore 0:
  31.4 49.3 all-gather.11
  261.7 82.0 all-reduce.10
  348.1 77.4 all-gather.7
  455.1 237.5 all-reduce.12
  698.9 83.2 all-reduce.14
  786.3 83.3 all-reduce.16
  873.2 24.8 all-gather.13
  900.1 78.6 all-gather.9
where the time goes:
time: 1010 us; the launch traced here: 1000 us
  waiting for transfers between devices  681 us (67%)
  other arithmetic  142 us (14%)
  matrix products  67.1 us (7%)
  blocking collectives  38.1 us (4%)
  local copies, waits for them, and re-layouts  37.7 us (4%)
  between operations  15.5 us (2%)
  starting transfers between devices  11.3 us (1%)
  loops' own time  10.5 us (1%)
    psum x2, waiting for transfers between devices, spread(): return lax.psum(jnp.where(mine, shard, jnp.zeros_like(shard)), axis)  320 us
    psum x2, waiting for transfers between devices, on_device(): carried = lax.psum(partial_sum, 'panel')  167 us
    all_gather x2, waiting for transfers between devices, on_device(): lax.all_gather(packed, 'panel', axis=0, tiled=True)  138 us
    another operation x14, other arithmetic, factor_block(): lower = jnp.linalg.cholesky(values)  78.6 us
    another operation x5, other arithmetic, factor_block(): lax.linalg.triangular_solve(lower, identity_block, left_side=True, lower=...  40 us
    dot_general x2, matrix products, outer_rows(): lax.dot_general(mine, piece, (((1,), (1,)), ((), ())), preferred_element_...  25.8 us
    all_to_all x1, blocking collectives, on_device(): lax.all_to_all(rows_out, 'panel', split_axis=0, concat_axis=0, tiled=True)  24.1 us
    all_gather x1, waiting for transfers between devices, on_device(): piece = lax.all_gather(front_values[None], 'front', axis=0, tiled=True)  23.5 us
  transfers between devices with their start and end apart: 10, of which 10 were waited for; matrix products, arithmetic and copies ran while one was open for 1% of the time, Pallas kernels for 0%

commit v1 on v0

--- a/solution.py
+++ b/solution.py
@@ -5,6 +5,27 @@
 
 K = 512
 NSTEP = 2
+
+
+def ring_gather(value, axis, dim):
+    length, mine, width = (lax.axis_size(axis), lax.axis_index(axis), value.shape[dim])
+    right = [(i, (i + 1) % length) for i in range(length)]
+    behind = [(i, (i - 1) % length) for i in range(length)]
+    out = jnp.zeros((*value.shape[:dim], length * width, *value.shape[dim + 1 :]), value.dtype)
+    out = lax.dynamic_update_slice_in_dim(out, value, mine * width, axis=dim)
+    from_left = from_right = value
+    half = length // 2
+    for hop in range(1, half + 1):
+        from_left = lax.ppermute(from_left, axis, right)
+        out = lax.dynamic_update_slice_in_dim(
+            out, from_left, (mine - hop) % length * width, axis=dim
+        )
+        if hop < length - half:
+            from_right = lax.ppermute(from_right, axis, behind)
+            out = lax.dynamic_update_slice_in_dim(
+                out, from_right, (mine + hop) % length * width, axis=dim
+            )
+    return out
 
 
 def spread(shard, axis, root):
@@ -81,7 +102,7 @@
         packed = column.astype(jnp.bfloat16)
         factors.append(column)
         inverses.append(inverse)
-        work = work - outer_rows(packed, lax.all_gather(packed, "panel", axis=0, tiled=True))
+        work = work - outer_rows(packed, ring_gather(packed, "panel", 0))
     factor_all = jnp.concatenate(factors, axis=1)
     trailing = work[:, pivots:]
     update_matrix = jnp.where(glob_rows[:, None] >= pivots, trailing, 0.0).astype(jnp.bfloat16)

time: 1010 us -> 1030 us (1.020)
  waiting for transfers between devices: 681 us -> 579 us
  starting transfers between devices: 11.3 us -> 83 us
  local copies, waits for them, and re-layouts: 37.7 us -> 95.8 us
    all_gather x2 -> x0, waiting for transfers between devices: 138 us -> none  [on_device(): lax.all_gather(packed, 'panel', axis=0, tiled=True)]
    ppermute x0 -> x30, waiting for transfers between devices: none -> 79.4 us  [the longest x16 79.1 us: ring_gather(): from_left = lax.ppermute(from_left, axis, right)]
    ppermute x0 -> x30, starting transfers between devices: none -> 71.8 us  [the longest x14 69.4 us: ring_gather(): from_right = lax.ppermute(from_right, axis, behind)]
    dynamic_update_slice x0 -> x30, local copies, waits for them, and re-layouts: none -> 45.3 us  [the longest x16 23.3 us: ring_gather(): lax.dynamic_update_slice_in_dim(out, from_left, (mine - hop) % length * w...]
    all_gather x1, waiting for transfers between devices: 23.5 us -> 0.01 us  [on_device(): piece = lax.all_gather(front_values[None], 'front', axis=0, tiled=True)]
    psum x2, waiting for transfers between devices: 320 us -> 306 us  [spread(): return lax.psum(jnp.where(mine, shard, jnp.zeros_like(shard)), axis)]
  transfers between devices with their start and end apart: 10 -> 38, of which waited for: 10 -> 17; matrix products, arithmetic and copies ran while one was open for 1% -> 8% of each run, Pallas kernels for 0% -> 0%
where the time goes in v1:
time: 1030 us
  waiting for transfers between devices  579 us (56%)
  other arithmetic  143 us (14%)
  local copies, waits for them, and re-layouts  95.8 us (9%)
  starting transfers between devices  83 us (8%)
  matrix products  62.1 us (6%)
  blocking collectives  38.1 us (4%)
  between operations  15.3 us (1%)
  loops' own time  12.1 us (1%)
    psum x2, waiting for transfers between devices, spread(): return lax.psum(jnp.where(mine, shard, jnp.zeros_like(shard)), axis)  306 us
    psum x2, waiting for transfers between devices, on_device(): carried = lax.psum(partial_sum, 'panel')  165 us
    ppermute x16, waiting for transfers between devices, ring_gather(): from_left = lax.ppermute(from_left, axis, right)  79.1 us
    another operation x14, other arithmetic, factor_block(): lower = jnp.linalg.cholesky(values)  78.8 us
    ppermute x14, starting transfers between devices, ring_gather(): from_right = lax.ppermute(from_right, axis, behind)  69.4 us
    another operation x5, other arithmetic, factor_block(): lax.linalg.triangular_solve(lower, identity_block, left_side=True, lower=...  40.3 us
    all_to_all x1, blocking collectives, on_device(): lax.all_to_all(rows_out, 'panel', split_axis=0, concat_axis=0, tiled=True)  24.1 us
    dynamic_update_slice x16, local copies, waits for them, and re-layouts, ring_gather(): lax.dynamic_update_slice_in_dim(out, from_left, (mine - hop) % length * w...  23.3 us
  transfers between devices with their start and end apart: 38, of which 17 were waited for; matrix products, arithmetic and copies ran while one was open for 8% of the time, Pallas kernels for 0%

profile of v1, /device:TPU:0, one launch (start us, length us, event | category | flops | bytes accessed | tf_op | source)
XLA Modules:
  0.0 1027.7 jit_solution(12366379211818486900)
XLA Ops:
  7.2 24.1 %all_to_all.19 = bf16[16,4,8192]{2,1,0:T(4,128)(2,1)} all-to-all(bf16[16,4,8192]{2,1,0:T(4,128)(2,1)} %bitcast.145), channel_id=1, replica_groups=mesh['front'=8,'panel'=16] {'panel'}, dimensions={0} | all-to-all | bytes 2097152 | tf_op jit(solution)/shard_map/all_to_all | solution.py:61
  44.0 14.0 %all-gather = s32[128,1,4]{2,1,0:T(1,128)S(1)} all-gather(s32[16,1,4]{2,1,0:T(1,128)S(1)} %all-to-all-done), channel_id=2, replica_groups=mesh['front'=8,'panel'=16] {'front'}, dimensions={0}, use_global_device_ids=true | all-gather | bytes 2304 | tf_op jit(solution)/shard_map/all_gather | solution.py:65
  58.0 22.9 %all-gather.6.cloned.1.call-done = bf16[128,4,8192]{2,1,0:T(4,128)(2,1)} async-done(((bf16[16,4,8192]{2,1,0:T(4,128)(2,1)}), bf16[128,4,8192]{2,1,0:T(4,128)(2,1)}) %all-gather.6.cloned.1.call-update) | async-done | bytes 8388624 | tf_op jit(solution)/shard_map/all_gather | solution.py:64
  80.9 24.2 %conditional.3 = (f32[512,8192]{1,0:T(8,128)}) conditional(s32[]{:T(128)} %convert_element_type.26, () %tuple.36, (pred[8]{0:T(512)(128)(4,1)S(1)}, s32[8,16,4]{2,1,0:T(8,128)S(1)}, s32[512]{0:T(512)S(1)}, bf16[8,16,4,8192]{3,2,1,0:T(4,128)(2,1)}) %tuple.135), branch_computations={%region_1.0_spmd, %region_2.3_spmd} | conditional | flops 4295229952 | bytes 41955344 | solution.py:75
  81.0 12.5 %reshape.120 = bf16[512,8192]{1,0:T(8,128)(2,1)} reshape(bf16[8,16,4,8192]{3,2,1,0:T(4,128)(2,1)} %get-tuple-element.54) | data formatting | bytes 16777216 | tf_op jit(solution)/shard_map/cond/branch_1_fun/reshape | solution.py:44
  93.6 11.5 %fusion = f32[512,8192]{1,0:T(8,128)} fusion(bf16[512,8192]{1,0:T(8,128)(2,1)} %reshape.120, s32[512]{0:T(512)S(1)} %eq.70, s32[512]{0:T(512)S(1)} %get-tuple-element.53), kind=kOutput, calls=%fused_computation | convolution fusion | flops 4295229440 | bytes 25169920 | tf_op jit(solution)/shard_map/cond/branch_1_fun/dot_general | solution.py:44
  117.9 144.3 %conditional.4 = (f32[512,512]{0,1:T(8,128)}) conditional(s32[]{:T(128)} %convert_element_type.27, () %tuple.38, (f32[512,512]{1,0:T(8,128)S(1)}, f32[512,512]{1,0:T(8,128)S(1)}) %tuple.39), branch_computations={%region_3.4_spmd, %region_4.15_spmd} | conditional | flops 1412760064 | bytes 26744084 | solution.py:98
  119.7 11.7 %cholesky.286 = f32[128,128]{1,0:T(8,128)S(1)} custom-call(f32[128,128]{1,0:T(8,128)S(1)} %cholesky.426), custom_call_target="Cholesky" | custom-call | tf_op jit(solution)/shard_map/cond/branch_1_fun/jit(cholesky)/cholesky | solution.py:84
  131.5 9.8 custom-call.27
  143.9 11.7 %cholesky.305 = f32[128,128]{1,0:T(8,128)S(1)} custom-call(f32[128,128]{1,0:T(8,128)S(1)} %cholesky.430), custom_call_target="Cholesky" | custom-call | tf_op jit(solution)/shard_map/cond/branch_1_fun/jit(cholesky)/cholesky | solution.py:84
  157.7 10.2 custom-call.28
  169.5 11.7 %cholesky.326 = f32[128,128]{1,0:T(8,128)S(1)} custom-call(f32[128,128]{1,0:T(8,128)S(1)} %cholesky.435), custom_call_target="Cholesky" | custom-call | tf_op jit(solution)/shard_map/cond/branch_1_fun/jit(cholesky)/cholesky | solution.py:84
  182.5 9.8 custom-call.29
  193.8 11.7 %cholesky.343 = f32[128,128]{1,0:T(8,128)S(1)} custom-call(f32[128,128]{1,0:T(8,128)S(1)} %convolution_subtract_fusion.5), custom_call_target="Cholesky" | custom-call | tf_op jit(solution)/shard_map/cond/branch_1_fun/jit(cholesky)/cholesky | solution.py:84
  206.9 10.4 %while.6 = (s32[]{:T(128)}, f32[512,512]{1,0:T(8,128)S(1)}, s32[4,2]{0,1:T(2,128)S(1)}, f32[4,128,128]{2,1,0:T(8,128)}, s32[]{:T(128)}) while((s32[]{:T(128)}, f32[512,512]{1,0:T(8,128)S(1)}, s32[4,2]{0,1:T(2,128)S(1)}, f32[4,128,128]{2,1,0:T(8,128)}, s32[]{:T(128)}) %tuple.111), condition=%wide.while_cond.2, body=%wide.while_body.2.sunk | while | flops 2 | bytes 132205 | solution.py:85
  217.4 40.1 %custom-call.30 = f32[4,128,128]{1,2,0:T(8,128)S(1)} custom-call(f32[4,128,128]{2,1,0:T(8,128)} %get-tuple-element.77), custom_call_target="InvertDiagBlocksLowerTriangular" | custom-call | tf_op jit(solution)/shard_map/cond/branch_1_fun/triangular_solve/custom-call.3 | solution.py:85
  264.6 82.1 %all-reduce.11.cloned.1.call-done = f32[512,512]{0,1:T(8,128)} async-done(((f32[512,512]{0,1:T(8,128)}), f32[512,512]{0,1:T(8,128)}) %all-reduce.11.cloned.1.call-update) | async-done | bytes 1048592 | tf_op jit(solution)/shard_map/psum | solution.py:33
  360.4 10.1 collective-permute-done
  375.8 9.2 collective-permute-done.2
  390.4 8.3 collective-permute-done.4
  404.8 7.4 collective-permute-done.6
  417.6 7.4 collective-permute-done.8
  467.5 13.9 %convolution_subtract_fusion.12 = f32[512,8192]{1,0:T(8,128)} fusion(f32[512,8192]{1,0:T(8,128)} %copy-done, bf16[512,512]{0,1:T(8,128)(2,1)S(1)} %get-tuple-element.132, bf16[8192,512]{0,1:T(8,128)(2,1)} %constant_dynamic-update-slice_fusion.24), kind=kOutput, calls=%fused_computation.141 | convolution fusion | flops 4299161600 | bytes 42467328 | tf_op jit(solution)/shard_map/dot_general | solution.py:37
  482.7 10.0 conditional.5
  494.0 224.3 %all-reduce.13.cloned.1.call-done = f32[512,512]{0,1:T(8,128)} async-done(((f32[512,512]{0,1:T(8,128)}), f32[512,512]{0,1:T(8,128)}) %all-reduce.13.cloned.1.call-update) | async-done | bytes 1048592 | tf_op jit(solution)/shard_map/psum | solution.py:33
  728.5 83.3 %all-reduce.15.cloned.1.call-done = f32[512,128]{1,0:T(8,128)} async-done(((f32[512,128]{1,0:T(8,128)}), f32[512,128]{1,0:T(8,128)}) %all-reduce.15.cloned.1.call-update) | async-done | bytes 262160 | tf_op jit(solution)/shard_map/psum | solution.py:126
  818.7 81.4 %all-reduce.17.cloned.1.call-done = f32[512,128]{1,0:T(8,128)} async-done(((f32[512,128]{1,0:T(8,128)}), f32[512,128]{1,0:T(8,128)}) %all-reduce.17.cloned.1.call-update) | async-done | bytes 262160 | tf_op jit(solution)/shard_map/psum | solution.py:126
  908.8 10.6 %collective-permute-done.17 = bf16[512,512]{0,1:T(8,128)(2,1)S(1)} collective-permute-done((bf16[512,512]{0,1:T(8,128)(2,1)}, bf16[512,512]{0,1:T(8,128)(2,1)S(1)}, u32[]{:S(2)}, u32[]{:S(2)}) %collective-permute-start.17) | collective-permute-done | bytes 524320 | tf_op jit(solution)/shard_map/ppermute | solution.py:19
  924.8 9.5 collective-permute-done.19
  939.6 8.6 collective-permute-done.21
  995.9 7.1 all-to-all-start.2
  1011.1 9.0 fusion.66
  (208 shorter events, 226.5 us)
Async XLA Ops:
  7.2 73.7 %all-gather.6.cloned.1.call-start = ((), (), s32[]{:S(2)}) async-start(), calls=%async_computation.7 | async-start | bytes 9437184 | tf_op jit(solution)/shard_map/all_gather | solution.py:64
  36.5 310.2 %all-reduce.11.cloned.1.call-start = ((), (), s32[]{:S(2)}) async-start(), calls=%async_computation.3 | async-start | bytes 2097152 | tf_op jit(solution)/shard_map/psum | solution.py:33
  264.5 453.7 %all-reduce.13.cloned.1.call-start = ((), (), s32[]{:S(2)}) async-start(), calls=%async_computation.4 | async-start | bytes 2097152 | tf_op jit(solution)/shard_map/psum | solution.py:33
  355.0 15.5 %collective-permute-start = (bf16[512,512]{0,1:T(8,128)(2,1)S(1)}, bf16[512,512]{0,1:T(8,128)(2,1)S(1)}, u32[]{:S(2)}, u32[]{:S(2)}) collective-permute-start(bf16[512,512]{0,1:T(8,128)(2,1)S(1)} %get-tuple-element.132), channel_id=1, source_target_pairs={{0,1},{1,2},{2,3},{3,4},{4,5},{5,6},{6,7},{7,8},{8,9},{9,10},{10,1... | collective-permute-start | bytes 1572872 | tf_op jit(solution)/shard_map/ppermute | solution.py:19
  356.0 14.5 %collective-permute-start.1 = (bf16[512,512]{0,1:T(8,128)(2,1)S(1)}, bf16[512,512]{0,1:T(8,128)(2,1)S(1)}, u32[]{:S(2)}, u32[]{:S(2)}) collective-permute-start(bf16[512,512]{0,1:T(8,128)(2,1)S(1)} %get-tuple-element.132), channel_id=1, source_target_pairs={{0,15},{1,0},{2,1},{3,2},{4,3},{5,4},{6,5},{7,6},{8,7},{9,8},{10,9... | collective-permute-start | bytes 1572872 | tf_op jit(solution)/shard_map/ppermute | solution.py:24
  370.5 14.5 %collective-permute-start.2 = (bf16[512,512]{0,1:T(8,128)(2,1)S(1)}, bf16[512,512]{0,1:T(8,128)(2,1)S(1)}, u32[]{:S(2)}, u32[]{:S(2)}) collective-permute-start(bf16[512,512]{0,1:T(8,128)(2,1)S(1)} %collective-permute-done), channel_id=1, source_target_pairs={{0,1},{1,2},{2,3},{3,4},{4,5},{5,6},{6,7},{7,8},{8,9},{9,10},{10,1... | collective-permute-start | bytes 1572872 | tf_op jit(solution)/shard_map/ppermute | solution.py:19
  370.5 14.5 %collective-permute-start.3 = (bf16[512,512]{0,1:T(8,128)(2,1)S(1)}, bf16[512,512]{0,1:T(8,128)(2,1)S(1)}, u32[]{:S(2)}, u32[]{:S(2)}) collective-permute-start(bf16[512,512]{0,1:T(8,128)(2,1)S(1)} %collective-permute-done.1), channel_id=1, source_target_pairs={{0,15},{1,0},{2,1},{3,2},{4,3},{5,4},{6,5},{7,6},{8,7},{9,8},{10,9... | collective-permute-start | bytes 1572872 | tf_op jit(solution)/shard_map/ppermute | solution.py:24
  385.0 13.6 %collective-permute-start.4 = (bf16[512,512]{0,1:T(8,128)(2,1)S(1)}, bf16[512,512]{0,1:T(8,128)(2,1)S(1)}, u32[]{:S(2)}, u32[]{:S(2)}) collective-permute-start(bf16[512,512]{0,1:T(8,128)(2,1)S(1)} %collective-permute-done.2), channel_id=1, source_target_pairs={{0,1},{1,2},{2,3},{3,4},{4,5},{5,6},{6,7},{7,8},{8,9},{9,10},{10,1... | collective-permute-start | bytes 1572872 | tf_op jit(solution)/shard_map/ppermute | solution.py:19
  385.1 14.4 %collective-permute-start.5 = (bf16[512,512]{0,1:T(8,128)(2,1)S(1)}, bf16[512,512]{0,1:T(8,128)(2,1)S(1)}, u32[]{:S(2)}, u32[]{:S(2)}) collective-permute-start(bf16[512,512]{0,1:T(8,128)(2,1)S(1)} %collective-permute-done.3), channel_id=1, source_target_pairs={{0,15},{1,0},{2,1},{3,2},{4,3},{5,4},{6,5},{7,6},{8,7},{9,8},{10,9... | collective-permute-start | bytes 1572872 | tf_op jit(solution)/shard_map/ppermute | solution.py:24
  412.2 17.6 %collective-permute-start.9 = (bf16[512,512]{0,1:T(8,128)(2,1)}, bf16[512,512]{0,1:T(8,128)(2,1)}, u32[]{:S(2)}, u32[]{:S(2)}) collective-permute-start(bf16[512,512]{0,1:T(8,128)(2,1)} %collective-permute-done.7), channel_id=1, source_target_pairs={{0,15},{1,0},{2,1},{3,2},{4,3},{5,4},{6,5},{7,6},{8,7},{9,8},{10,9... | collective-permute-start | bytes 1572872 | tf_op jit(solution)/shard_map/ppermute | solution.py:24
  425.0 14.1 %collective-permute-start.10 = (bf16[512,512]{0,1:T(8,128)(2,1)}, bf16[512,512]{0,1:T(8,128)(2,1)}, u32[]{:S(2)}, u32[]{:S(2)}) collective-permute-start(bf16[512,512]{0,1:T(8,128)(2,1)} %collective-permute-done.8), channel_id=1, source_target_pairs={{0,1},{1,2},{2,3},{3,4},{4,5},{5,6},{6,7},{7,8},{8,9},{9,10},{10,1... | collective-permute-start | bytes 1572872 | tf_op jit(solution)/shard_map/ppermute | solution.py:19
  429.8 17.1 %collective-permute-start.11 = (bf16[512,512]{0,1:T(8,128)(2,1)}, bf16[512,512]{0,1:T(8,128)(2,1)S(1)}, u32[]{:S(2)}, u32[]{:S(2)}) collective-permute-start(bf16[512,512]{0,1:T(8,128)(2,1)} %collective-permute-done.9), channel_id=1, source_target_pairs={{0,15},{1,0},{2,1},{3,2},{4,3},{5,4},{6,5},{7,6},{8,7},{9,8},{10,9... | collective-permute-start | bytes 1572872 | tf_op jit(solution)/shard_map/ppermute | solution.py:24
  439.1 15.0 %collective-permute-start.12 = (bf16[512,512]{0,1:T(8,128)(2,1)}, bf16[512,512]{0,1:T(8,128)(2,1)S(1)}, u32[]{:S(2)}, u32[]{:S(2)}) collective-permute-start(bf16[512,512]{0,1:T(8,128)(2,1)} %collective-permute-done.10), channel_id=1, source_target_pairs={{0,1},{1,2},{2,3},{3,4},{4,5},{5,6},{6,7},{7,8},{8,9},{9,10},{10,1... | collective-permute-start | bytes 1572872 | tf_op jit(solution)/shard_map/ppermute | solution.py:19
  446.9 12.9 %collective-permute-start.13 = (bf16[512,512]{0,1:T(8,128)(2,1)S(1)}, bf16[512,512]{0,1:T(8,128)(2,1)S(1)}, u32[]{:S(2)}, u32[]{:S(2)}) collective-permute-start(bf16[512,512]{0,1:T(8,128)(2,1)S(1)} %collective-permute-done.11), channel_id=1, source_target_pairs={{0,15},{1,0},{2,1},{3,2},{4,3},{5,4},{6,5},{7,6},{8,7},{9,8},{10,9... | collective-permute-start | bytes 1572872 | tf_op jit(solution)/shard_map/ppermute | solution.py:24
  493.8 317.9 %all-reduce.15.cloned.1.call-start = ((), (), s32[]{:S(2)}) async-start(), calls=%async_computation.5 | async-start | bytes 524288 | tf_op jit(solution)/shard_map/psum | solution.py:126
  728.4 171.7 %all-reduce.17.cloned.1.call-start = ((), (), s32[]{:S(2)}) async-start(), calls=%async_computation.6 | async-start | bytes 524288 | tf_op jit(solution)/shard_map/psum | solution.py:126
  815.9 174.7 %all-gather.8.cloned.1.call-start = ((), (), s32[]{:S(2)}) async-start(), calls=%async_computation.8 | async-start | bytes 2359296 | tf_op jit(solution)/shard_map/all_gather | solution.py:136
  815.9 88.7 %collective-permute-start.16 = (bf16[512,512]{0,1:T(8,128)(2,1)S(1)}, bf16[512,512]{0,1:T(8,128)(2,1)}, u32[]{:S(2)}, u32[]{:S(2)}) collective-permute-start(bf16[512,512]{0,1:T(8,128)(2,1)S(1)} %get-tuple-element.130), channel_id=1, source_target_pairs={{0,15},{1,0},{2,1},{3,2},{4,3},{5,4},{6,5},{7,6},{8,7},{9,8},{10,9... | collective-permute-start | bytes 1572872 | tf_op jit(solution)/shard_map/ppermute | solution.py:24
  818.7 84.7 %collective-permute-start.15 = (bf16[512,512]{0,1:T(8,128)(2,1)S(1)}, bf16[512,512]{0,1:T(8,128)(2,1)}, u32[]{:S(2)}, u32[]{:S(2)}) collective-permute-start(bf16[512,512]{0,1:T(8,128)(2,1)S(1)} %get-tuple-element.130), channel_id=1, source_target_pairs={{0,1},{1,2},{2,3},{3,4},{4,5},{5,6},{6,7},{7,8},{8,9},{9,10},{10,1... | collective-permute-start | bytes 1572872 | tf_op jit(solution)/shard_map/ppermute | solution.py:19
  903.4 16.0 %collective-permute-start.17 = (bf16[512,512]{0,1:T(8,128)(2,1)}, bf16[512,512]{0,1:T(8,128)(2,1)S(1)}, u32[]{:S(2)}, u32[]{:S(2)}) collective-permute-start(bf16[512,512]{0,1:T(8,128)(2,1)} %collective-permute-done.15), channel_id=1, source_target_pairs={{0,1},{1,2},{2,3},{3,4},{4,5},{5,6},{6,7},{7,8},{8,9},{9,10},{10,1... | collective-permute-start | bytes 1572872 | tf_op jit(solution)/shard_map/ppermute | solution.py:19
  904.6 14.8 %collective-permute-start.18 = (bf16[512,512]{0,1:T(8,128)(2,1)}, bf16[512,512]{0,1:T(8,128)(2,1)S(1)}, u32[]{:S(2)}, u32[]{:S(2)}) collective-permute-start(bf16[512,512]{0,1:T(8,128)(2,1)} %collective-permute-done.16), channel_id=1, source_target_pairs={{0,15},{1,0},{2,1},{3,2},{4,3},{5,4},{6,5},{7,6},{8,7},{9,8},{10,9... | collective-permute-start | bytes 1572872 | tf_op jit(solution)/shard_map/ppermute | solution.py:24
  919.4 14.8 %collective-permute-start.19 = (bf16[512,512]{0,1:T(8,128)(2,1)S(1)}, bf16[512,512]{0,1:T(8,128)(2,1)S(1)}, u32[]{:S(2)}, u32[]{:S(2)}) collective-permute-start(bf16[512,512]{0,1:T(8,128)(2,1)S(1)} %collective-permute-done.17), channel_id=1, source_target_pairs={{0,1},{1,2},{2,3},{3,4},{4,5},{5,6},{6,7},{7,8},{8,9},{9,10},{10,1... | collective-permute-start | bytes 1572872 | tf_op jit(solution)/shard_map/ppermute | solution.py:19
  919.4 14.8 %collective-permute-start.20 = (bf16[512,512]{0,1:T(8,128)(2,1)S(1)}, bf16[512,512]{0,1:T(8,128)(2,1)}, u32[]{:S(2)}, u32[]{:S(2)}) collective-permute-start(bf16[512,512]{0,1:T(8,128)(2,1)S(1)} %collective-permute-done.18), channel_id=1, source_target_pairs={{0,15},{1,0},{2,1},{3,2},{4,3},{5,4},{6,5},{7,6},{8,7},{9,8},{10,9... | collective-permute-start | bytes 1572872 | tf_op jit(solution)/shard_map/ppermute | solution.py:24
  934.2 14.0 %collective-permute-start.21 = (bf16[512,512]{0,1:T(8,128)(2,1)S(1)}, bf16[512,512]{0,1:T(8,128)(2,1)}, u32[]{:S(2)}, u32[]{:S(2)}) collective-permute-start(bf16[512,512]{0,1:T(8,128)(2,1)S(1)} %collective-permute-done.19), channel_id=1, source_target_pairs={{0,1},{1,2},{2,3},{3,4},{4,5},{5,6},{6,7},{7,8},{8,9},{9,10},{10,1... | collective-permute-start | bytes 1572872 | tf_op jit(solution)/shard_map/ppermute | solution.py:19
  935.0 13.9 %collective-permute-start.22 = (bf16[512,512]{0,1:T(8,128)(2,1)}, bf16[512,512]{0,1:T(8,128)(2,1)}, u32[]{:S(2)}, u32[]{:S(2)}) collective-permute-start(bf16[512,512]{0,1:T(8,128)(2,1)} %collective-permute-done.20), channel_id=1, source_target_pairs={{0,15},{1,0},{2,1},{3,2},{4,3},{5,4},{6,5},{7,6},{8,7},{9,8},{10,9... | collective-permute-start | bytes 1572872 | tf_op jit(solution)/shard_map/ppermute | solution.py:24
  948.2 14.3 %collective-permute-start.23 = (bf16[512,512]{0,1:T(8,128)(2,1)}, bf16[512,512]{0,1:T(8,128)(2,1)}, u32[]{:S(2)}, u32[]{:S(2)}) collective-permute-start(bf16[512,512]{0,1:T(8,128)(2,1)} %collective-permute-done.21), channel_id=1, source_target_pairs={{0,1},{1,2},{2,3},{3,4},{4,5},{5,6},{6,7},{7,8},{8,9},{9,10},{10,1... | collective-permute-start | bytes 1572872 | tf_op jit(solution)/shard_map/ppermute | solution.py:19
  948.9 15.8 %collective-permute-start.24 = (bf16[512,512]{0,1:T(8,128)(2,1)}, bf16[512,512]{0,1:T(8,128)(2,1)}, u32[]{:S(2)}, u32[]{:S(2)}) collective-permute-start(bf16[512,512]{0,1:T(8,128)(2,1)} %collective-permute-done.22), channel_id=1, source_target_pairs={{0,15},{1,0},{2,1},{3,2},{4,3},{5,4},{6,5},{7,6},{8,7},{9,8},{10,9... | collective-permute-start | bytes 1572872 | tf_op jit(solution)/shard_map/ppermute | solution.py:24
  962.5 13.1 %collective-permute-start.25 = (bf16[512,512]{0,1:T(8,128)(2,1)}, bf16[512,512]{0,1:T(8,128)(2,1)S(1)}, u32[]{:S(2)}, u32[]{:S(2)}) collective-permute-start(bf16[512,512]{0,1:T(8,128)(2,1)} %collective-permute-done.23), channel_id=1, source_target_pairs={{0,1},{1,2},{2,3},{3,4},{4,5},{5,6},{6,7},{7,8},{8,9},{9,10},{10,1... | collective-permute-start | bytes 1572872 | tf_op jit(solution)/shard_map/ppermute | solution.py:19
  964.6 12.9 %collective-permute-start.26 = (bf16[512,512]{0,1:T(8,128)(2,1)}, bf16[512,512]{0,1:T(8,128)(2,1)S(1)}, u32[]{:S(2)}, u32[]{:S(2)}) collective-permute-start(bf16[512,512]{0,1:T(8,128)(2,1)} %collective-permute-done.24), channel_id=1, source_target_pairs={{0,15},{1,0},{2,1},{3,2},{4,3},{5,4},{6,5},{7,6},{8,7},{9,8},{10,9... | collective-permute-start | bytes 1572872 | tf_op jit(solution)/shard_map/ppermute | solution.py:24
  975.6 12.9 %collective-permute-start.27 = (bf16[512,512]{0,1:T(8,128)(2,1)S(1)}, bf16[512,512]{0,1:T(8,128)(2,1)S(1)}, u32[]{:S(2)}, u32[]{:S(2)}) collective-permute-start(bf16[512,512]{0,1:T(8,128)(2,1)S(1)} %collective-permute-done.25), channel_id=1, source_target_pairs={{0,1},{1,2},{2,3},{3,4},{4,5},{5,6},{6,7},{7,8},{8,9},{9,10},{10,1... | collective-permute-start | bytes 1572872 | tf_op jit(solution)/shard_map/ppermute | solution.py:19
  988.5 14.5 %collective-permute-start.29 = (bf16[512,512]{0,1:T(8,128)(2,1)S(1)}, bf16[512,512]{0,1:T(8,128)(2,1)S(1)}, u32[]{:S(2)}, u32[]{:S(2)}) collective-permute-start(bf16[512,512]{0,1:T(8,128)(2,1)S(1)} %collective-permute-done.27), channel_id=1, source_target_pairs={{0,1},{1,2},{2,3},{3,4},{4,5},{5,6},{6,7},{7,8},{8,9},{9,10},{10,1... | collective-permute-start | bytes 1572872 | tf_op jit(solution)/shard_map/ppermute | solution.py:19
  995.9 24.2 %all-to-all-start.2 = ((f32[16,4,128]{2,1,0:T(4,128)}), f32[16,4,128]{2,1,0:T(4,128)S(1)}, u32[]{:S(2)}, u32[]{:S(2)}) async-start(f32[16,4,128]{2,1,0:T(4,128)} %copy.36), calls=%async_computation.2 | async-start | bytes 65536 | tf_op jit(solution)/shard_map/all_to_all | solution.py:141
  (21 other events, 721.6 us)
Sparse Core Ops, SparseCore 0:
  31.4 49.3 all-gather.5
  264.6 82.0 all-reduce.10
  493.9 224.2 all-reduce.12
  728.5 83.1 all-reduce.14
  816.0 84.0 all-reduce.16
  903.5 24.7 all-gather.7
